TPU v7x, 256 devices: a whole 4x4x8 slice. The times are simulated.
256 devices in a mesh: dp: 32 (over z, y), chan: 8 (over x, core).
Axes of the slice: x: 4, y: 4, z: 8, core: 2. Of those that a mesh axis runs over, the one named last changes fastest.
Arguments:
- inputs: bfloat16 [12544, 2048], P('dp', 'chan'), may hold values from -6 to 6
- conv_one: bfloat16 [9, 32, 2048], P(None, None, 'chan'), may hold values from -0.375 to 0.375
- conv_two: bfloat16 [9, 32, 2048], P(None, None, 'chan'), may hold values from -0.375 to 0.375
- probe_one: bfloat16 [2048, 512], P('chan'), may hold values from -0.125 to 0.125
- probe_two: bfloat16 [2048, 512], P('chan'), may hold values from -0.125 to 0.125
Outputs:
- restored: bfloat16 [12544, 2048], P('dp', 'chan')
- triangle: float32 [512, 512], replicated
All inputs are finite; a program needn't handle non-finite values.
Results may differ from a plain program's by a relative error of at most 0.028.
Values may be sent and summed in bfloat16 or wider, within the bound.
No kernel may reach another device: no remote copies, remote signals or barrier semaphores. Data moves between devices by JAX's collectives and lax.ppermute only.
A program may use at most 64 MiB of HBM per device.

v0:
```python
import math

import jax
import jax.numpy as jnp
from jax import lax
from jax.sharding import PartitionSpec as P

SIDE = 7


def convolve(field, weight):
    pixels, width = field.shape
    group_width = weight.shape[1]
    groups = width // group_width
    images = field.reshape(pixels // (SIDE * SIDE), SIDE, SIDE, width)
    padded = jnp.pad(images, ((0, 0), (1, 1), (1, 1), (0, 0)))
    total = jnp.zeros((pixels, groups, group_width), jnp.float32)
    for offset in range(9):
        row_shift = offset // 3
        col_shift = offset % 3
        window = padded[:, row_shift : row_shift + SIDE, col_shift : col_shift + SIDE, :]
        window = window.reshape(pixels, groups, group_width)
        kernel = weight[offset].reshape(group_width, groups, group_width)
        total = total + jnp.einsum(
            "pgi,igo->pgo", window, kernel, preferred_element_type=jnp.float32
        )
    return total.reshape(pixels, width).astype(jnp.bfloat16)


def gram_of(sketch):
    return lax.dot_general(
        sketch, sketch, (((0,), (0,)), ((), ())), preferred_element_type=jnp.float32
    )


def cross_of(sketch, responses):
    return lax.dot_general(
        sketch, responses, (((0,), (0,)), ((), ())), preferred_element_type=jnp.float32
    )


def finish(sketch, gram, cross):
    lower = jnp.linalg.cholesky(gram)
    coeffs = lax.linalg.triangular_solve(lower, cross, left_side=True, lower=True).astype(
        jnp.bfloat16
    )
    mapped = lax.linalg.triangular_solve(
        lower, coeffs.astype(jnp.float32), left_side=True, lower=True, transpose_a=True
    ).astype(jnp.bfloat16)
    return (jnp.dot(sketch, mapped, preferred_element_type=jnp.float32).astype(jnp.bfloat16), lower)


def compress(responses, probe):
    partial_sketch = jnp.dot(responses, probe, preferred_element_type=jnp.float32)
    sketch = lax.psum(partial_sketch, "chan").astype(jnp.bfloat16)
    gram, cross = lax.psum((gram_of(sketch), cross_of(sketch, responses)), "dp")
    return finish(sketch, gram, cross)


def per_device(inputs, conv_one, conv_two, probe_one, probe_two):
    responses_one = convolve(inputs, conv_one)
    restored_one, lower_one = compress(responses_one, probe_one)
    activated = jnp.maximum(restored_one, jnp.zeros((), jnp.bfloat16))
    responses_two = convolve(activated, conv_two)
    restored, lower_two = compress(responses_two, probe_two)
    total_rows = inputs.shape[0] * lax.axis_size("dp")
    triangle = jnp.transpose(lower_two) * (1.0 / math.sqrt(total_rows))
    return (restored, triangle)


def solution(mesh):
    in_specs = (
        P("dp", "chan"),
        P(None, None, "chan"),
        P(None, None, "chan"),
        P("chan", None),
        P("chan", None),
    )
    out_specs = (P("dp", "chan"), P())
    return jax.shard_map(
        per_device, mesh=mesh, in_specs=in_specs, out_specs=out_specs, check_vma=False
    )
```

profile of v0, /device:TPU:1, one launch (start us, length us, event | category | flops | bytes accessed | tf_op | source)
XLA Modules:
  0.0 702.6 jit_solution(17671794830554544109)
XLA Ops:
  12.0 1.2 reshape.119
  13.9 1.3 reshape.120
  18.1 1.2 reshape.124
  20.1 1.2 reshape.123
  22.1 1.4 reshape.121
  23.5 1.3 fusion.29
  31.8 29.7 %all-reduce.13 = bf16[392,512]{1,0:T(8,128)(2,1)S(1)} all-reduce(f32[392,512]{1,0:T(8,128)S(1)} %fusion.143), channel_id=1, replica_groups=mesh['dp'=32,'chan'=8] {'chan'}, use_global_device_ids=true, to_apply=%region_0.1 | all-reduce | flops 200704 | bytes 1204224 | tf_op jit(solution)/shard_map/psum | solution.py:55
  62.7 1.5 fusion.149
  71.0 144.7 %all-reduce.12.cloned.1.call-done = (f32[512,256]{1,0:T(8,128)}, f32[512,512]{0,1:T(8,128)}) async-done(((f32[512,256]{1,0:T(8,128)}, f32[512,512]{0,1:T(8,128)}), (f32[512,256]{1,0:T(8,128)}, f32[512,512]{0,1:T(8,128)})) %all-reduce.12.cloned.1.call-update) | async-done | bytes 1572880 | tf_op jit(solution)/shard_map/psum | solution.py:56
  215.6 1.6 copy.60
  218.5 11.7 %cholesky.286 = f32[128,128]{1,0:T(8,128)S(1)} custom-call(f32[128,128]{1,0:T(8,128)S(1)} %cholesky.426), custom_call_target="Cholesky" | custom-call | tf_op jit(solution)/shard_map/jit(cholesky)/cholesky | solution.py:43
  230.4 9.8 %custom-call.31 = f32[1,128,128]{1,2,0:T(8,128)S(1)} custom-call(f32[1,128,128]{2,1,0:T(8,128)S(1)} %get-tuple-element.120), custom_call_target="InvertDiagBlocksLowerTriangular" | custom-call | tf_op jit(solution)/shard_map/jit(cholesky)/cholesky | solution.py:43
  240.9 11.7 %cholesky.305 = f32[128,128]{1,0:T(8,128)S(1)} custom-call(f32[128,128]{1,0:T(8,128)S(1)} %cholesky.430), custom_call_target="Cholesky" | custom-call | tf_op jit(solution)/shard_map/jit(cholesky)/cholesky | solution.py:43
  252.6 10.2 %custom-call.32 = f32[1,128,128]{1,2,0:T(8,128)S(1)} custom-call(f32[1,128,128]{2,1,0:T(8,128)S(1)} %get-tuple-element.117), custom_call_target="InvertDiagBlocksLowerTriangular" | custom-call | tf_op jit(solution)/shard_map/jit(cholesky)/cholesky | solution.py:43
  263.5 11.7 %cholesky.326 = f32[128,128]{1,0:T(8,128)S(1)} custom-call(f32[128,128]{1,0:T(8,128)S(1)} %cholesky.435), custom_call_target="Cholesky" | custom-call | tf_op jit(solution)/shard_map/jit(cholesky)/cholesky | solution.py:43
  276.0 9.8 %custom-call.33 = f32[1,128,128]{1,2,0:T(8,128)S(1)} custom-call(f32[1,128,128]{2,1,0:T(8,128)S(1)} %get-tuple-element.114), custom_call_target="InvertDiagBlocksLowerTriangular" | custom-call | tf_op jit(solution)/shard_map/jit(cholesky)/cholesky | solution.py:43
  286.4 11.9 %cholesky.343 = f32[128,128]{1,0:T(8,128)S(1)} custom-call(f32[128,128]{1,0:T(8,128)S(1)} %convolution_subtract_fusion.17), custom_call_target="Cholesky" | custom-call | tf_op jit(solution)/shard_map/jit(cholesky)/cholesky | solution.py:43
  302.3 8.4 %while.8 = (s32[]{:T(128)}, f32[512,512]{1,0:T(8,128)S(1)}, s32[4,2]{0,1:T(2,128)S(1)}, f32[4,128,128]{2,1,0:T(8,128)S(1)}, s32[]{:T(128)}) while((s32[]{:T(128)}, f32[512,512]{1,0:T(8,128)S(1)}, s32[4,2]{0,1:T(2,128)S(1)}, f32[4,128,128]{2,1,0:T(8,128)S(1)}, s32[]{:T(128)}) %tuple.96), condition=%wide.while_cond.1, body=%wide.while_body.1.sunk | while | flops 2 | bytes 131181 | solution.py:47
  303.0 1.4 bitcast_dynamic-update-slice_fusion.4
  305.1 1.4 bitcast_dynamic-update-slice_fusion.4
  307.2 1.4 bitcast_dynamic-update-slice_fusion.4
  309.3 1.4 bitcast_dynamic-update-slice_fusion.4
  310.7 39.3 %custom-call.35 = f32[4,128,128]{1,2,0:T(8,128)S(1)} custom-call(f32[4,128,128]{2,1,0:T(8,128)S(1)} %get-tuple-element.34), custom_call_target="InvertDiagBlocksLowerTriangular" | custom-call | tf_op jit(solution)/shard_map/triangular_solve/custom-call.8 | solution.py:47
  357.1 1.2 reshape.129
  358.3 1.2 reshape.130
  359.9 1.3 reshape.133
  361.2 1.2 reshape.134
  362.8 1.4 reshape.136
  364.2 1.4 fusion.20
  373.2 31.2 %all-reduce.14 = bf16[392,512]{1,0:T(8,128)(2,1)S(1)} all-reduce(f32[392,512]{1,0:T(8,128)S(1)} %fusion.145), channel_id=1, replica_groups=mesh['dp'=32,'chan'=8] {'chan'}, use_global_device_ids=true, to_apply=%region_11.15 | all-reduce | flops 200704 | bytes 1204224 | tf_op jit(solution)/shard_map/psum | solution.py:55
  404.4 1.5 fusion.147
  405.9 1.2 fusion.146
  407.1 145.7 %all-reduce.10.cloned.1.call-done = (f32[512,256]{1,0:T(8,128)}, f32[512,512]{0,1:T(8,128)}) async-done(((f32[512,256]{1,0:T(8,128)}, f32[512,512]{0,1:T(8,128)}), (f32[512,256]{1,0:T(8,128)}, f32[512,512]{0,1:T(8,128)})) %all-reduce.10.cloned.1.call-update) | async-done | bytes 1572880 | tf_op jit(solution)/shard_map/psum | solution.py:56
  552.8 1.6 copy.80
  555.6 11.7 %cholesky.358 = f32[128,128]{1,0:T(8,128)S(1)} custom-call(f32[128,128]{1,0:T(8,128)S(1)} %cholesky.439), custom_call_target="Cholesky" | custom-call | tf_op jit(solution)/shard_map/jit(cholesky)/cholesky | solution.py:43
  567.5 9.8 %custom-call.36 = f32[1,128,128]{1,2,0:T(8,128)S(1)} custom-call(f32[1,128,128]{2,1,0:T(8,128)S(1)} %get-tuple-element.110), custom_call_target="InvertDiagBlocksLowerTriangular" | custom-call | tf_op jit(solution)/shard_map/jit(cholesky)/cholesky | solution.py:43
  578.0 11.7 %cholesky.377 = f32[128,128]{1,0:T(8,128)S(1)} custom-call(f32[128,128]{1,0:T(8,128)S(1)} %cholesky.443), custom_call_target="Cholesky" | custom-call | tf_op jit(solution)/shard_map/jit(cholesky)/cholesky | solution.py:43
  591.0 9.9 %custom-call.37 = f32[1,128,128]{1,2,0:T(8,128)S(1)} custom-call(f32[1,128,128]{2,1,0:T(8,128)S(1)} %get-tuple-element.107), custom_call_target="InvertDiagBlocksLowerTriangular" | custom-call | tf_op jit(solution)/shard_map/jit(cholesky)/cholesky | solution.py:43
  601.6 11.7 %cholesky.398 = f32[128,128]{1,0:T(8,128)S(1)} custom-call(f32[128,128]{1,0:T(8,128)S(1)} %cholesky.448), custom_call_target="Cholesky" | custom-call | tf_op jit(solution)/shard_map/jit(cholesky)/cholesky | solution.py:43
  614.1 9.8 %custom-call.38 = f32[1,128,128]{1,2,0:T(8,128)S(1)} custom-call(f32[1,128,128]{2,1,0:T(8,128)S(1)} %get-tuple-element.104), custom_call_target="InvertDiagBlocksLowerTriangular" | custom-call | tf_op jit(solution)/shard_map/jit(cholesky)/cholesky | solution.py:43
  624.5 11.9 %cholesky.415 = f32[128,128]{1,0:T(8,128)S(1)} custom-call(f32[128,128]{1,0:T(8,128)S(1)} %convolution_subtract_fusion.16), custom_call_target="Cholesky" | custom-call | tf_op jit(solution)/shard_map/jit(cholesky)/cholesky | solution.py:43
  640.9 8.4 %while.9 = (s32[]{:T(128)}, f32[512,512]{1,0:T(8,128)S(1)}, s32[4,2]{0,1:T(2,128)S(1)}, f32[4,128,128]{2,1,0:T(8,128)S(1)}, s32[]{:T(128)}) while((s32[]{:T(128)}, f32[512,512]{1,0:T(8,128)S(1)}, s32[4,2]{0,1:T(2,128)S(1)}, f32[4,128,128]{2,1,0:T(8,128)S(1)}, s32[]{:T(128)}) %tuple.108), condition=%wide.while_cond.1.clone, body=%wide.while_body.1.clone.sunk | while | flops 2 | bytes 131181 | solution.py:47
  641.6 1.4 bitcast_dynamic-update-slice_fusion.5
  643.7 1.4 bitcast_dynamic-update-slice_fusion.5
  645.8 1.4 bitcast_dynamic-update-slice_fusion.5
  647.9 1.4 bitcast_dynamic-update-slice_fusion.5
  649.3 39.3 %custom-call.40 = f32[4,128,128]{1,2,0:T(8,128)S(1)} custom-call(f32[4,128,128]{2,1,0:T(8,128)S(1)} %get-tuple-element.36), custom_call_target="InvertDiagBlocksLowerTriangular" | custom-call | tf_op jit(solution)/shard_map/triangular_solve/custom-call.8 | solution.py:47
  694.2 1.3 copy.81
  (222 shorter events, 63.3 us)
Async XLA Ops:
  7.2 24.3 %copy-start = (bf16[256,512]{1,0:T(8,128)(2,1)S(1)}, bf16[256,512]{1,0:T(8,128)(2,1)}, u32[]{:S(2)}) copy-start(bf16[256,512]{1,0:T(8,128)(2,1)} %param.13) | copy-start | bytes 786436
  7.2 1.1 copy-start.18
  7.2 208.4 %all-reduce.12.cloned.1.call-start = ((), (), s32[]{:S(2)}) async-start(), calls=%async_computation.1 | async-start | bytes 3145728 | tf_op jit(solution)/shard_map/psum | solution.py:56
  8.3 0.9 copy-start.36
  23.5 1.3 copy-start.22
  24.9 0.8 copy-start.23
  25.3 1.2 copy-start.4
  25.7 0.9 copy-start.24
  26.1 1.2 copy-start.5
  26.6 0.9 copy-start.25
  27.5 0.9 copy-start.16
  27.5 1.0 copy-start.28
  27.5 1.3 copy-start.6
  28.4 0.9 copy-start.34
  29.3 1.1 copy-start.7
  29.4 1.1 copy-start.35
  64.1 0.9 copy-start.37
  64.1 488.6 %all-reduce.10.cloned.1.call-start = ((), (), s32[]{:S(2)}) async-start(), calls=%async_computation | async-start | bytes 3145728 | tf_op jit(solution)/shard_map/psum | solution.py:56
  215.6 1.7 copy-start.1
  217.5 1.0 copy-start.14
  218.5 21.7 %copy-start.15 = (f32[512,512]{1,0:T(8,128)S(1)}, f32[512,512]{1,0:T(8,128)}, u32[]{:S(2)}) copy-start(f32[512,512]{1,0:T(8,128)} %copy-done.14) | copy-start | bytes 3145732
  302.2 47.9 %copy-start.19 = (f32[512,256]{1,0:T(8,128)S(1)}, f32[512,256]{1,0:T(8,128)}, u32[]{:S(2)}) copy-start(f32[512,256]{1,0:T(8,128)} %get-tuple-element.59) | copy-start | bytes 1572868
  364.2 1.4 copy-start.17
  364.2 1.4 copy-start.27
  364.2 1.6 copy-start.11
  365.6 0.8 copy-start.33
  366.4 1.1 copy-start.10
  366.4 1.1 copy-start.32
  367.6 0.8 copy-start.21
  368.4 1.1 copy-start.9
  368.4 1.1 copy-start.31
  369.6 1.1 copy-start.8
  369.6 1.1 copy-start.30
  370.7 0.8 copy-start.29
  372.0 1.0 copy-start.26
  552.8 1.7 copy-start.2
  554.6 1.0 copy-start.12
  555.6 21.7 %copy-start.13 = (f32[512,512]{1,0:T(8,128)S(1)}, f32[512,512]{1,0:T(8,128)}, u32[]{:S(2)}) copy-start(f32[512,512]{1,0:T(8,128)} %copy-done.12) | copy-start | bytes 3145732
  639.7 48.9 %copy-start.20 = (f32[512,256]{1,0:T(8,128)S(1)}, f32[512,256]{1,0:T(8,128)}, u32[]{:S(2)}) copy-start(f32[512,256]{1,0:T(8,128)} %get-tuple-element.57) | copy-start | bytes 1572868
  693.0 1.2 copy-start.3
Sparse Core Ops, SparseCore 0:
  64.3 151.3 all-reduce.11
  407.2 145.5 all-reduce.9
where the time goes:
time: 713 us; the launch traced here: 703 us
  waiting for transfers between devices  290 us (41%)
  other arithmetic  239 us (34%)
  local copies, waits for them, and re-layouts  62.7 us (9%)
  blocking collectives  60.9 us (9%)
  matrix products  29 us (4%)
  between operations  20.4 us (3%)
    psum x2, waiting for transfers between devices, compress(): gram, cross = lax.psum((gram_of(sketch), cross_of(sketch, responses)), 'dp')  290 us
    another operation x29, other arithmetic, finish(): lower = jnp.linalg.cholesky(gram)  158 us
    another operation x4, other arithmetic, finish(): lax.linalg.triangular_solve(lower, coeffs.astype(jnp.float32), left_side=...  78.8 us
    psum x2, blocking collectives, compress(): sketch = lax.psum(partial_sketch, 'chan').astype(jnp.bfloat16)  60.9 us
    another operation x27, local copies, waits for them, and re-layouts, finish(): lax.linalg.triangular_solve(lower, coeffs.astype(jnp.float32), left_side=...  16.6 us
    reshape x16, local copies, waits for them, and re-layouts, convolve(): window = window.reshape(pixels, groups, group_width)  14.8 us
  transfers between devices with their start and end apart: 2, of which 2 were waited for; matrix products, arithmetic and copies ran while one was open for 1% of the time, Pallas kernels for 0%

commit v1 on v0

v1 whole, which is shorter than its diff:
```python
import functools
import math

import jax
import jax.numpy as jnp
from jax import lax
from jax.experimental import pallas as pl
from jax.experimental.pallas import tpu as pltpu
from jax.sharding import Mesh, PartitionSpec as P

SIDE = 7
K = 512
NB = 128
HALF = 256
F32 = jnp.float32
BF16 = jnp.bfloat16
HI = lax.Precision.HIGHEST
VMEM = pl.BlockSpec(memory_space=pltpu.VMEM)
SMEM = pl.BlockSpec(memory_space=pltpu.SMEM)
PARAMS = pltpu.CompilerParams(vmem_limit_bytes=48 << 20)
BLOCKS = (((0, 0), (0, 1), (0, 2), (0, 3), (1, 1)), ((1, 2), (1, 3), (2, 2), (2, 3), (3, 3)))
NG = 5 * NB


def dot(a, b, dims=((1,), (0,)), precision=None):
    return lax.dot_general(
        a, b, (dims, ((), ())), precision=precision, preferred_element_type=F32
    )


def bcast_lane(x, k):
    return jnp.broadcast_to(x[:, k : k + 1], (8, NB))


def bcast_row(x, k):
    return jnp.broadcast_to(x[k : k + 1, :], (8, NB))


def factor(rows):
    n = len(rows)
    sub = lax.broadcasted_iota(jnp.int32, (8, NB), 0)
    lane = lax.broadcasted_iota(jnp.int32, (8, NB), 1)
    inv = [(lane == sub + 8 * r).astype(F32) for r in range(n)]
    rows = list(rows)
    upper, lower_inv = [], []
    for r in range(n):
        top, top_inv = rows[r], inv[r]
        cols = [bcast_lane(top, 8 * r + k) for k in range(8)]
        s = {(i, k): bcast_row(cols[k], i) for k in range(8) for i in range(k, 8)}
        m, d = {}, []
        for k in range(8):
            d.append(s[k, k])
            over = 1.0 / s[k, k]
            for i in range(k + 1, 8):
                m[i, k] = s[i, k] * over
            for j in range(k + 1, 8):
                for i in range(j, 8):
                    s[i, j] = s[i, j] - m[i, k] * s[j, k]
        t = {}
        for j in range(8):
            for i in range(j + 1, 8):
                v = m[i, j]
                for k in range(j + 1, i):
                    v = v + m[i, k] * t[k, j]
                t[i, j] = -v
        q = [lax.rsqrt(x) for x in d]
        u = v = None
        for j in range(8):
            c = jnp.where(sub == j, q[j], 0.0)
            for i in range(j + 1, 8):
                c = jnp.where(sub == i, q[i] * t[i, j], c)
            uj, vj = c * bcast_row(top, j), c * bcast_row(top_inv, j)
            u, v = (uj, vj) if u is None else (u + uj, v + vj)
        upper.append(jnp.where(lane >= 8 * r + sub, u, 0.0))
        lower_inv.append(v)
        ub = [bcast_row(u, k) for k in range(8)]
        vb = [bcast_row(v, k) for k in range(8)]
        for g in range(r + 1, n):
            cg = [bcast_lane(rows[g], 8 * r + k) for k in range(8)]
            a, w = rows[g], inv[g]
            for k in range(8):
                l = cg[k]
                for j in range(k):
                    l = l + t[k, j] * cg[j]
                l = q[k] * l
                a, w = a - l * ub[k], w - l * vb[k]
            rows[g], inv[g] = a, w
    return upper, lower_inv


def solve_body(core, pack_ref, other_ref, lt_ref, a_ref, v_ref, g_ref):
    mine = pl.multiple_of(core * NG, NG)
    theirs = pl.multiple_of((1 - core) * NG, NG)
    g_ref[pl.ds(mine, NG), :] = pack_ref[:NG, :]
    g_ref[pl.ds(theirs, NG), :] = other_ref[...]
    for c in range(2):
        for n, (i, j) in enumerate(BLOCKS[c]):
            p = (5 * c + n) * NB
            a_ref[i * NB : (i + 1) * NB, j * NB : (j + 1) * NB] = g_ref[p : p + NB, :]
    for h in range(2):
        p = NG + h * K
        a_ref[:, K + h * NB : K + (h + 1) * NB] = pack_ref[p : p + K, :]
    lt_ref[...] = jnp.zeros(lt_ref.shape, F32)
    for b in range(4):
        o = b * NB
        u, v = factor([a_ref[o + 8 * i : o + 8 * i + 8, o : o + NB] for i in range(16)])
        for i in range(16):
            lt_ref[o + 8 * i : o + 8 * i + 8, o : o + NB] = u[i]
            v_ref[o + 8 * i : o + 8 * i + 8, :] = v[i]
        vb = v_ref[o : o + NB, :]
        if b < 3:
            lt_ref[o : o + NB, o + NB : K] = dot(vb, a_ref[o : o + NB, o + NB : K], precision=HI)
        a_ref[o : o + NB, K:] = dot(vb, a_ref[o : o + NB, K:], precision=HI)
        for r in range(b + 1, 4):
            p = r * NB
            ubr = lt_ref[o : o + NB, p : p + NB]
            a_ref[p : p + NB, p:K] -= dot(ubr, lt_ref[o : o + NB, p:K], ((0,), (0,)), HI)
            a_ref[p : p + NB, K:] -= dot(ubr, a_ref[o : o + NB, K:], ((0,), (0,)), HI)
    xs = [None] * 4
    for b in (3, 2, 1, 0):
        o = b * NB
        y = a_ref[o : o + NB, K:].astype(BF16).astype(F32)
        for c in range(b + 1, 4):
            y = y - dot(lt_ref[o : o + NB, c * NB : (c + 1) * NB], xs[c], precision=HI)
        xs[b] = dot(v_ref[o : o + NB, :], y, ((0,), (0,)), HI)
    return [x.astype(BF16) for x in xs]


def conv_body(core, w_ref, p_ref, r_ref, keep_ref, send_ref, pad_ref, win_ref, bd_ref):
    n = r_ref.shape[0]
    width = r_ref.shape[1]
    group = w_ref.shape[1]
    row = lax.broadcasted_iota(jnp.int32, (n, width), 0)
    q = lax.rem(row, SIDE * SIDE)
    y, x = lax.div(q, SIDE), lax.rem(q, SIDE)
    bi = lax.broadcasted_iota(jnp.int32, (width, width), 0)
    bj = lax.broadcasted_iota(jnp.int32, (width, width), 1)
    same = lax.div(bi, group) == lax.div(bj, group)
    for tap in range(9):
        a, b = tap // 3 - 1, tap % 3 - 1
        d = 8 + a * SIDE + b
        window = pad_ref[d : d + n, :]
        ok = None
        if a:
            ok = (y > 0) if a < 0 else (y < SIDE - 1)
        if b:
            okx = (x > 0) if b < 0 else (x < SIDE - 1)
            ok = okx if ok is None else ok & okx
        if ok is not None:
            window = jnp.where(ok, window, 0.0)
        win_ref[:, tap * width : (tap + 1) * width] = window.astype(BF16)
        tiled = jnp.concatenate([w_ref[tap].astype(F32)] * (width // group), axis=0)
        bd_ref[tap * width : (tap + 1) * width, :] = jnp.where(same, tiled, 0.0).astype(BF16)
    r = dot(win_ref[...], bd_ref[...]).astype(BF16)
    r_ref[...] = r
    mine = pl.multiple_of(core * HALF, HALF)
    theirs = pl.multiple_of((1 - core) * HALF, HALF)
    send_ref[...] = dot(r, p_ref[:, pl.ds(theirs, HALF)]).astype(BF16)
    keep_ref[...] = dot(r, p_ref[:, pl.ds(mine, HALF)])


def pad_field(pad_ref, field):
    n, width = field.shape
    pad_ref[0:8, :] = jnp.zeros((8, width), F32)
    pad_ref[8 + n : 16 + n, :] = jnp.zeros((8, width), F32)
    pad_ref[8 : 8 + n, :] = field


def first_kernel(core_ref, f_ref, w_ref, p_ref, r_ref, keep_ref, send_ref, pad_ref, win_ref, bd_ref):
    pad_field(pad_ref, f_ref[...].astype(F32))
    conv_body(core_ref[0], w_ref, p_ref, r_ref, keep_ref, send_ref, pad_ref, win_ref, bd_ref)


def middle_kernel(core_ref, pack_ref, other_ref, s_ref, w_ref, p_ref, r_ref, keep_ref, send_ref,
                  lt_ref, a_ref, v_ref, g_ref, pad_ref, win_ref, bd_ref):
    core = core_ref[0]
    xs = solve_body(core, pack_ref, other_ref, lt_ref, a_ref, v_ref, g_ref)
    restored = dot(s_ref[...], jnp.concatenate(xs, axis=0)).astype(BF16).astype(F32)
    pad_field(pad_ref, jnp.maximum(restored, 0.0))
    conv_body(core, w_ref, p_ref, r_ref, keep_ref, send_ref, pad_ref, win_ref, bd_ref)


def last_kernel(scale, core_ref, pack_ref, other_ref, s_ref, out_ref, tri_ref,
                lt_ref, a_ref, v_ref, g_ref):
    xs = solve_body(core_ref[0], pack_ref, other_ref, lt_ref, a_ref, v_ref, g_ref)
    tri_ref[...] = lt_ref[...] * scale
    out_ref[...] = dot(s_ref[...], jnp.concatenate(xs, axis=0)).astype(BF16)


def gram_kernel(core_ref, own_ref, other_ref, r_ref, s_ref, m_ref):
    core = core_ref[0]
    s_ref[:, pl.ds(pl.multiple_of(core * HALF, HALF), HALF)] = own_ref[...]
    s_ref[:, pl.ds(pl.multiple_of((1 - core) * HALF, HALF), HALF)] = other_ref[...]
    s = s_ref[...]
    cross = dot(s, r_ref[...], ((0,), (0,)))
    for h in range(2):
        m_ref[NG + h * K : NG + (h + 1) * K, :] = cross[:, h * NB : (h + 1) * NB]
    m_ref[NG + 2 * K :, :] = jnp.zeros((NB, NB), F32)
    for c in range(2):

        @pl.when(core == c)
        def _():
            for n, (i, j) in enumerate(BLOCKS[c]):
                block = dot(
                    s_ref[:, i * NB : (i + 1) * NB], s_ref[:, j * NB : (j + 1) * NB], ((0,), (0,))
                )
                m_ref[n * NB : (n + 1) * NB, :] = block


def solve_scratch():
    return [
        pltpu.VMEM((K, K), F32),
        pltpu.VMEM((K, K + HALF), F32),
        pltpu.VMEM((K, NB), F32),
        pltpu.VMEM((2 * NG, NB), F32),
    ]


def conv_scratch(n, width):
    return [
        pltpu.VMEM((n + 16, width), F32),
        pltpu.VMEM((n, 9 * width), BF16),
        pltpu.VMEM((9 * width, width), BF16),
    ]


def conv_outs(n, width):
    return (
        jax.ShapeDtypeStruct((n, width), BF16),
        jax.ShapeDtypeStruct((n, HALF), F32),
        jax.ShapeDtypeStruct((n, HALF), BF16),
    )


def call(kernel, name, outs, args, scratch=()):
    return pl.pallas_call(
        kernel,
        out_shape=outs,
        in_specs=[SMEM] + [VMEM] * (len(args) - 1),
        out_specs=jax.tree.map(lambda _: VMEM, outs),
        scratch_shapes=list(scratch),
        compiler_params=PARAMS,
        name=name,
    )(*args)


SWAP = ((0, 1), (1, 0))


def spread(x, axes):
    n = lax.axis_size(axes)
    return lax.all_to_all(jnp.broadcast_to(x[None], (n,) + x.shape), axes, 0, 0)


def sketch_of(keep, send):
    pair = (keep + lax.ppermute(send, "core", SWAP).astype(F32)).astype(BF16)
    own = jnp.sum(spread(pair, "x").astype(F32), axis=0).astype(BF16)
    return own, lax.ppermute(own, "core", SWAP)


def reduce_pack(m):
    n = lax.axis_size(("z", "y"))
    parts = lax.all_to_all(m.reshape(n, m.shape[0] // n, NB), ("z", "y"), 0, 0)
    pack = spread(jnp.sum(parts, axis=0), ("z", "y")).reshape(m.shape)
    return pack, lax.ppermute(pack[:NG], "core", SWAP)


def compress_sums(core, r, keep, send):
    own, other = sketch_of(keep, send)
    n = r.shape[0]
    outs = (
        jax.ShapeDtypeStruct((n, K), BF16),
        jax.ShapeDtypeStruct((NG + 2 * K + NB, NB), F32),
    )
    s, m = call(gram_kernel, "gram", outs, (core, own, other, r))
    pack, gram_other = reduce_pack(m)
    return pack, gram_other, s


def per_device(inputs, conv_one, conv_two, probe_one, probe_two):
    n, width = inputs.shape
    total_rows = n * lax.axis_size(("z", "y"))
    core = lax.axis_index("core").astype(jnp.int32).reshape(1)
    outs = conv_outs(n, width)
    r, keep, send = call(
        first_kernel, "first", outs, (core, inputs, conv_one, probe_one), conv_scratch(n, width)
    )
    sums = compress_sums(core, r, keep, send)
    r, keep, send = call(
        middle_kernel, "middle", outs, (core, *sums, conv_two, probe_two),
        solve_scratch() + conv_scratch(n, width),
    )
    sums = compress_sums(core, r, keep, send)
    outs = (jax.ShapeDtypeStruct((n, width), BF16), jax.ShapeDtypeStruct((K, K), F32))
    return call(
        functools.partial(last_kernel, 1.0 / math.sqrt(total_rows)), "last", outs, (core, *sums),
        solve_scratch(),
    )


def solution(mesh):
    grid = Mesh(mesh.devices.reshape(8, 4, 4, 2), ("z", "y", "x", "core"))
    rows, chan = ("z", "y"), ("x", "core")
    in_specs = (
        P(rows, chan),
        P(None, None, chan),
        P(None, None, chan),
        P(chan, None),
        P(chan, None),
    )
    out_specs = (P(rows, chan), P())
    return jax.shard_map(
        per_device, mesh=grid, in_specs=in_specs, out_specs=out_specs, check_vma=False
    )
```

time: 713 us -> 239 us (0.34)
  waiting for transfers between devices: 290 us -> 6.81 us
  other arithmetic: 239 us -> 0.57 us
  blocking collectives: 60.9 us -> 151 us
  local copies, waits for them, and re-layouts: 62.7 us -> 3.06 us
  Pallas kernels: 0 us -> 59 us
  matrix products: 29 us -> 0 us
  between operations: 20.4 us -> 0.95 us
  starting transfers between devices: 0.26 us -> 13.2 us
    psum x2 -> x0, waiting for transfers between devices: 290 us -> none  [compress(): gram, cross = lax.psum((gram_of(sketch), cross_of(sketch, responses)), 'dp')]
    another operation x33 -> x0, other arithmetic: 237 us -> none  [the longest x29 158 us: finish(): lower = jnp.linalg.cholesky(gram)]
    all_to_all x0 -> x6, blocking collectives: none -> 151 us  [the longest x4 87.5 us: spread(): return lax.all_to_all(jnp.broadcast_to(x[None], (n,) + x.shape), axes, 0, 0)]
    psum x2 -> x0, blocking collectives: 60.9 us -> none  [compress(): sketch = lax.psum(partial_sketch, 'chan').astype(jnp.bfloat16)]
    pallas_call x0 -> x5, Pallas kernels: none -> 59 us  [call(): pl.pallas_call(kernel, out_shape=outs, in_specs=[SMEM] + [VMEM] * (len(ar...]
    another operation x35 -> x0, local copies, waits for them, and re-layouts: 16.9 us -> none  [the longest x27 16.6 us: finish(): lax.linalg.triangular_solve(lower, coeffs.astype(jnp.float32), left_side=...]
    dot_general x26 -> x0, matrix products: 16.4 us -> none  [the longest x18 9.41 us: convolve(): jnp.einsum('pgi,igo->pgo', window, kernel, preferred_element_type=jnp.flo...]
    reshape x18 -> x0, local copies, waits for them, and re-layouts: 16 us -> none  [the longest x16 14.8 us: convolve(): window = window.reshape(pixels, groups, group_width)]
  transfers between devices with their start and end apart: 2 -> 6, of which waited for: 2 -> 6; matrix products, arithmetic and copies ran while one was open for 1% -> 0% of each run, Pallas kernels for 0% -> 0%
where the time goes in v1:
time: 239 us; the launch traced here: 235 us
  blocking collectives  151 us (63%)
  Pallas kernels  59 us (25%)
  starting transfers between devices  13.2 us (6%)
  waiting for transfers between devices  6.81 us (3%)
  local copies, waits for them, and re-layouts  3.06 us (1%)
    all_to_all x4, blocking collectives, spread(): return lax.all_to_all(jnp.broadcast_to(x[None], (n,) + x.shape), axes, 0, 0)  87.5 us
    all_to_all x2, blocking collectives, reduce_pack(): parts = lax.all_to_all(m.reshape(n, m.shape[0] // n, NB), ('z', 'y'), 0, 0)  63.6 us
    pallas_call x5, Pallas kernels, call(): pl.pallas_call(kernel, out_shape=outs, in_specs=[SMEM] + [VMEM] * (len(ar...  59 us
    ppermute x2, starting transfers between devices, reduce_pack(): return (pack, lax.ppermute(pack[:NG], 'core', SWAP))  6.88 us
  transfers between devices with their start and end apart: 6, of which 6 were waited for; matrix products, arithmetic and copies ran while one was open for 0% of the time, Pallas kernels for 0%

profile of v1, /device:TPU:1, one launch (start us, length us, event | category | flops | bytes accessed | tf_op | source)
XLA Modules:
  0.0 234.8 jit_solution(7558325304585118174)
XLA Ops:
  0.6 0.0 copy-start.1
  0.6 0.9 copy-done.1
  1.6 0.0 copy-start.2
  1.6 0.9 copy-done.2
  2.5 0.0 copy-start.4
  2.5 0.9 copy-done.4
  3.4 1.1 first.1
  4.5 3.3 %collective-permute-start = (bf16[392,256]{1,0:T(8,128)(2,1)S(1)}, bf16[392,256]{1,0:T(8,128)(2,1)S(1)}, u32[]{:S(2)}, u32[]{:S(2)}) collective-permute-start(bf16[392,256]{1,0:T(8,128)(2,1)S(1)} %get-tuple-element.13), channel_id=1, source_target_pairs={{0,1},{1,0},{2,3},{3,2},{4,5},{5,4},{6,7},{7,6},{8,9},{9,8},{10,11... | collective-permute-start | bytes 602120 | tf_op jit(solution)/shard_map/ppermute | solution.py:256
  7.9 1.1 collective-permute-done
  9.0 0.1 add_convert_fusion.1
  9.0 0.1 broadcast_in_dim.8
  9.1 14.6 %all_to_all.30 = bf16[4,392,256]{2,1,0:T(8,128)(2,1)S(1)} all-to-all(bf16[4,392,256]{2,1,0:T(8,128)(2,1)S(1)} %broadcast_in_dim.8), channel_id=1, replica_groups=mesh['z'=8,'y'=4,'x'=4,'core'=2] {'x'}, dimensions={0} | all-to-all | bytes 1605632 | tf_op jit(solution)/shard_map/all_to_all | solution.py:252
  23.7 0.2 reduce_sum.42.own_ref
  23.8 1.3 collective-permute-start.1
  25.1 1.1 collective-permute-done.1.other_ref
  26.2 0.8 gram.2
  27.0 34.7 %all_to_all.31 = f32[32,56,128]{2,1,0:T(8,128)S(1)} all-to-all(f32[32,56,128]{2,1,0:T(8,128)S(1)} %bitcast.9), channel_id=1, replica_groups=mesh['z'=8,'y'=4,'x'=4,'core'=2] {'z','y'}, dimensions={0} | all-to-all | bytes 1835008 | tf_op jit(solution)/shard_map/all_to_all | solution.py:263
  61.7 0.1 reduce_sum.43
  61.7 0.1 broadcast_in_dim.9
  61.8 29.2 %all_to_all.32 = f32[32,56,128]{2,1,0:T(8,128)S(1)} all-to-all(f32[32,56,128]{2,1,0:T(8,128)S(1)} %broadcast_in_dim.9), channel_id=1, replica_groups=mesh['z'=8,'y'=4,'x'=4,'core'=2] {'z','y'}, dimensions={0} | all-to-all | bytes 1835008 | tf_op jit(solution)/shard_map/all_to_all | solution.py:252
  91.0 0.0 copy-start
  91.0 0.0 copy-start.3
  91.0 3.4 %collective-permute-start.2 = (f32[640,128]{1,0:T(8,128)S(1)}, f32[640,128]{1,0:T(8,128)S(1)}, u32[]{:S(2)}, u32[]{:S(2)}) collective-permute-start(f32[640,128]{1,0:T(8,128)S(1)} %slice.8), channel_id=1, source_target_pairs={{0,1},{1,0},{2,3},{3,2},{4,5},{5,4},{6,7},{7,6},{8,9},{9,8},{10,11... | collective-permute-start | bytes 983048 | tf_op jit(solution)/shard_map/ppermute | solution.py:265
  94.4 1.3 collective-permute-done.2.other_ref
  95.7 0.0 copy-done
  95.7 0.0 copy-done.3
  95.7 28.4 %middle.1 = (bf16[392,256]{1,0:T(8,128)(2,1)S(1)}, f32[392,256]{1,0:T(8,128)S(1)}, bf16[392,256]{1,0:T(8,128)(2,1)S(1)}) custom-call(s32[1]{0:T(128)} %bitcast.core_ref, f32[1792,128]{1,0:T(8,128)S(1)} %bitcast.6, f32[640,128]{1,0:T(8,128)S(1)} %collective-permute-done.2.other_ref, bf16[392,512]{1,0:T(8,128)(2,1)S(1)} %get-tuple-element.16.s_ref, ...), custom_call_target="tpu_custom_call" | custom-call | tf_op jit(solution)/shard_map/middle/pallas_call | solution.py:236
  124.1 0.5 collective-permute-start.3
  124.6 1.1 collective-permute-done.3
  125.6 0.1 add_convert_fusion
  125.7 0.1 broadcast_in_dim.10
  125.8 14.6 %all_to_all.33 = bf16[4,392,256]{2,1,0:T(8,128)(2,1)S(1)} all-to-all(bf16[4,392,256]{2,1,0:T(8,128)(2,1)S(1)} %broadcast_in_dim.10), channel_id=1, replica_groups=mesh['z'=8,'y'=4,'x'=4,'core'=2] {'x'}, dimensions={0} | all-to-all | bytes 1605632 | tf_op jit(solution)/shard_map/all_to_all | solution.py:252
  140.4 0.2 reduce_sum.44.own_ref
  140.5 1.3 collective-permute-start.4
  141.8 1.1 collective-permute-done.4.other_ref
  142.9 0.8 gram.3
  143.7 28.9 %all_to_all.34 = f32[32,56,128]{2,1,0:T(8,128)S(1)} all-to-all(f32[32,56,128]{2,1,0:T(8,128)S(1)} %bitcast.10), channel_id=1, replica_groups=mesh['z'=8,'y'=4,'x'=4,'core'=2] {'z','y'}, dimensions={0} | all-to-all | bytes 1835008 | tf_op jit(solution)/shard_map/all_to_all | solution.py:263
  172.6 0.1 reduce_sum.45
  172.7 0.1 broadcast_in_dim.11
  172.7 29.2 %all_to_all.35 = f32[32,56,128]{2,1,0:T(8,128)S(1)} all-to-all(f32[32,56,128]{2,1,0:T(8,128)S(1)} %broadcast_in_dim.11), channel_id=1, replica_groups=mesh['z'=8,'y'=4,'x'=4,'core'=2] {'z','y'}, dimensions={0} | all-to-all | bytes 1835008 | tf_op jit(solution)/shard_map/all_to_all | solution.py:252
  201.9 3.4 %collective-permute-start.5 = (f32[640,128]{1,0:T(8,128)S(1)}, f32[640,128]{1,0:T(8,128)S(1)}, u32[]{:S(2)}, u32[]{:S(2)}) collective-permute-start(f32[640,128]{1,0:T(8,128)S(1)} %slice.9), channel_id=1, source_target_pairs={{0,1},{1,0},{2,3},{3,2},{4,5},{5,4},{6,7},{7,6},{8,9},{9,8},{10,11... | collective-permute-start | bytes 983048 | tf_op jit(solution)/shard_map/ppermute | solution.py:265
  205.4 1.3 collective-permute-done.5.other_ref
  206.6 27.9 %last.1 = (bf16[392,256]{1,0:T(8,128)(2,1)}, f32[512,512]{1,0:T(8,128)}) custom-call(s32[1]{0:T(128)} %bitcast.core_ref, f32[1792,128]{1,0:T(8,128)S(1)} %bitcast.8, f32[640,128]{1,0:T(8,128)S(1)} %collective-permute-done.5.other_ref, bf16[392,512]{1,0:T(8,128)(2,1)S(1)} %get-tuple-element.21.s_ref), custom_call_target="tpu_custom_call" | custom-call | tf_op jit(solution)/shard_map/last/pallas_call | solution.py:236
  (2 shorter events, 0.0 us)
Async XLA Ops:
  0.6 1.0 copy-start.1
  1.6 0.9 copy-start.2
  2.5 0.9 copy-start.4
  4.5 4.4 %collective-permute-start = (bf16[392,256]{1,0:T(8,128)(2,1)S(1)}, bf16[392,256]{1,0:T(8,128)(2,1)S(1)}, u32[]{:S(2)}, u32[]{:S(2)}) collective-permute-start(bf16[392,256]{1,0:T(8,128)(2,1)S(1)} %get-tuple-element.13), channel_id=1, source_target_pairs={{0,1},{1,0},{2,3},{3,2},{4,5},{5,4},{6,7},{7,6},{8,9},{9,8},{10,11... | collective-permute-start | bytes 602120 | tf_op jit(solution)/shard_map/ppermute | solution.py:256
  23.8 2.4 %collective-permute-start.1 = (bf16[392,256]{1,0:T(8,128)(2,1)S(1)}, bf16[392,256]{1,0:T(8,128)(2,1)S(1)}, u32[]{:S(2)}, u32[]{:S(2)}) collective-permute-start(bf16[392,256]{1,0:T(8,128)(2,1)S(1)} %reduce_sum.42.own_ref), channel_id=1, source_target_pairs={{0,1},{1,0},{2,3},{3,2},{4,5},{5,4},{6,7},{7,6},{8,9},{9,8},{10,11... | collective-permute-start | bytes 602120 | tf_op jit(solution)/shard_map/ppermute | solution.py:258
  91.0 4.7 %copy-start = (bf16[256,512]{1,0:T(8,128)(2,1)S(1)}, bf16[256,512]{1,0:T(8,128)(2,1)}, u32[]{:S(2)}) copy-start(bf16[256,512]{1,0:T(8,128)(2,1)} %p_ref.3) | copy-start | bytes 786436
  91.0 4.7 %copy-start.3 = (bf16[9,32,256]{2,1,0:T(8,128)(2,1)S(1)}, bf16[9,32,256]{2,1,0:T(8,128)(2,1)}, u32[]{:S(2)}) copy-start(bf16[9,32,256]{2,1,0:T(8,128)(2,1)} %w_ref.3) | copy-start | bytes 442372
  91.0 4.7 %collective-permute-start.2 = (f32[640,128]{1,0:T(8,128)S(1)}, f32[640,128]{1,0:T(8,128)S(1)}, u32[]{:S(2)}, u32[]{:S(2)}) collective-permute-start(f32[640,128]{1,0:T(8,128)S(1)} %slice.8), channel_id=1, source_target_pairs={{0,1},{1,0},{2,3},{3,2},{4,5},{5,4},{6,7},{7,6},{8,9},{9,8},{10,11... | collective-permute-start | bytes 983048 | tf_op jit(solution)/shard_map/ppermute | solution.py:265
  124.1 1.5 collective-permute-start.3
  140.5 2.4 %collective-permute-start.4 = (bf16[392,256]{1,0:T(8,128)(2,1)S(1)}, bf16[392,256]{1,0:T(8,128)(2,1)S(1)}, u32[]{:S(2)}, u32[]{:S(2)}) collective-permute-start(bf16[392,256]{1,0:T(8,128)(2,1)S(1)} %reduce_sum.44.own_ref), channel_id=1, source_target_pairs={{0,1},{1,0},{2,3},{3,2},{4,5},{5,4},{6,7},{7,6},{8,9},{9,8},{10,11... | collective-permute-start | bytes 602120 | tf_op jit(solution)/shard_map/ppermute | solution.py:258
  201.9 4.7 %collective-permute-start.5 = (f32[640,128]{1,0:T(8,128)S(1)}, f32[640,128]{1,0:T(8,128)S(1)}, u32[]{:S(2)}, u32[]{:S(2)}) collective-permute-start(f32[640,128]{1,0:T(8,128)S(1)} %slice.9), channel_id=1, source_target_pairs={{0,1},{1,0},{2,3},{3,2},{4,5},{5,4},{6,7},{7,6},{8,9},{9,8},{10,11... | collective-permute-start | bytes 983048 | tf_op jit(solution)/shard_map/ppermute | solution.py:265
